TPU v7x, 128 devices: a whole 4x4x4 slice. The times are simulated.
128 devices in a mesh: obs: 8 (over z_hi, y), unk: 16 (over z_lo, x, core).
Axes of the slice: x: 4, y: 4, z: 4 (z_hi: 2, z_lo: 2; z = z_hi * 2 + z_lo), core: 2. Of those that a mesh axis runs over, the one named last changes fastest.
Arguments:
- design: float32 [8192, 24576], P('obs', 'unk'), may hold values from -0.0625 to 0.0625
- weights: float32 [8192], P('obs'), may hold values from 0.25 to 4
Outputs:
- factor: float32 [24576, 1024], P(('unk', 'obs'))
All inputs are finite; a program needn't handle non-finite values.
Results may differ from a plain program's by a relative error of at most 0.00011.
Values sent between devices are 32-bit elements; how exact they have to be, the bound alone decides.
No kernel may reach another device: no remote copies, remote signals or barrier semaphores. Data moves between devices by JAX's collectives and lax.ppermute only.
A program may use at most 128 MiB of HBM per device.

v0:
```python
import jax, jax.numpy as jnp
from jax import lax
from jax.experimental import pallas as pl
from jax.experimental.pallas import tpu as pltpu
from jax.sharding import PartitionSpec as P

BLOCK = 128
SUB = 8
STRIP = 64


def split(x):
    hi = x.astype(jnp.bfloat16)
    return hi, (x - hi.astype(jnp.float32)).astype(jnp.bfloat16)


def dot_t(a, b):
    return lax.dot_general(a, b, (((1,), (1,)), ((), ())), preferred_element_type=jnp.float32)


def dot3_t(a, b):
    (ah, al), (bh, bl) = a, b
    return dot_t(ah, bh) + (dot_t(ah, bl) + dot_t(al, bh))


def on_lanes(value, lane):
    return jnp.broadcast_to(value[:, lane : lane + 1], (SUB, BLOCK))


def invert_diag(block_ref, inv_ref, stage, rows_ref):
    lane = lax.broadcasted_iota(jnp.int32, (SUB, BLOCK), 1)
    panels = BLOCK // SUB
    groups = [block_ref[q * SUB : (q + 1) * SUB, :] for q in range(panels)]
    natural, carried = None, None
    for p in range(panels):
        r0 = p * SUB
        base = (p % 2) * 3 * SUB * SUB
        one = lambda row: stage[pl.ds(base + row, SUB, stride=0), :]
        panel = groups[p]
        columns = [on_lanes(panel, r0 + c) for c in range(SUB)]
        if natural is not None:
            for i in range(SUB):
                stage[base + i * SUB : base + (i + 1) * SUB, :] = on_lanes(natural, r0 + i)
            panel = jnp.where((lane >= r0 - SUB) & (lane < r0), 0.0, panel)
            for k in range(SUB):
                down = stage[pl.ds(base + k, SUB, stride=SUB), :]
                panel = panel - down * carried[k]
                for c in range(SUB):
                    columns[c] = columns[c] - down * one(c * SUB + k)
        inside = (lane >= r0) & (lane < r0 + SUB)
        sub = lax.broadcasted_iota(jnp.int32, (SUB, BLOCK), 0)
        panel = jnp.where(inside, jnp.where(lane == r0 + sub, 1.0, 0.0), panel)
        at = SUB * SUB
        for c in range(SUB):
            stage[base + at + c * SUB : base + at + (c + 1) * SUB, :] = columns[c]
        stage[base + 2 * at : base + 2 * at + SUB, :] = panel
        e = {(i, c): one(at + c * SUB + i) for c in range(SUB) for i in range(c + 1)}
        w = [one(2 * at + i) for i in range(SUB)]
        for c in range(SUB):
            inv = lax.rsqrt(e[c, c])
            w[c] = w[c] * inv
            u = {i: e[c, i] * inv for i in range(c + 1, SUB)}
            for i in range(c + 1, SUB):
                w[i] = w[i] - u[i] * w[c]
                for j in range(i, SUB):
                    e[i, j] = e[i, j] - u[i] * u[j]
            rows_ref[r0 + c : r0 + c + 1, :] = w[c][0:1, :]
        natural, carried = rows_ref[r0 : r0 + SUB, :], w
        inv_ref[r0 : r0 + SUB, :] = jnp.where(lane < r0 + SUB, natural, 0.0)
        if p + 2 < panels:
            for q in range(p + 2, panels):
                spare = 6 * SUB * SUB + (q % 2) * SUB * SUB
                for i in range(SUB):
                    stage[spare + i * SUB : spare + (i + 1) * SUB, :] = on_lanes(natural, q * SUB + i)
                groups[q] = jnp.where(inside, 0.0, groups[q])
                for k in range(SUB):
                    groups[q] = groups[q] - stage[pl.ds(spare + k, SUB, stride=SUB), :] * w[k]


def unpack(where_ref, mine_ref, other_ref, work, pieces):
    count = mine_ref.shape[0]
    chip, core = where_ref[0], where_ref[1]
    for k in range(count):
        pieces[2 * (chip ^ k) + core] = mine_ref[k]
        pieces[2 * (chip ^ k) + 1 - core] = other_ref[k]
    for t in range(2 * count):
        low, high = t * STRIP, (4 * count - 1 - t) * STRIP
        cut, rest = (low // BLOCK + 1) * BLOCK, (high // BLOCK + 1) * BLOCK
        work[low : low + STRIP, :cut] = pieces[t, :, :cut]
        work[high : high + STRIP, :rest] = pieces[t, :, cut:]


def chol_kernel(where_ref, mine_ref, other_ref, low_ref, inv_ref, work, pieces, diag, dinv, left_ref, right_ref, stage, rows_ref):
    work[...] = jnp.zeros_like(work)
    unpack(where_ref, mine_ref, other_ref, work, pieces)
    factor_steps(low_ref, inv_ref, work, diag, dinv, left_ref, right_ref, stage, rows_ref)


def factor_steps(low_ref, inv_ref, work, diag, dinv, left_ref, right_ref, stage, rows_ref):
    width = work.shape[0]
    blocks = width // BLOCK
    left_ref[...] = jnp.zeros_like(left_ref)
    right_ref[...] = jnp.zeros_like(right_ref)

    def step(k, _):
        at = pl.multiple_of(k * BLOCK, BLOCK)
        after = pl.multiple_of(jnp.minimum(k + 1, blocks - 1) * BLOCK, BLOCK)
        diag[...] = work[pl.ds(at, BLOCK), pl.ds(at, BLOCK)]
        for i in range(blocks):
            rows = slice(i * BLOCK, (i + 1) * BLOCK)
            work[rows, :] = work[rows, :] - dot_t(left_ref[rows, :], right_ref[...])
        invert_diag(diag, dinv, stage, rows_ref)
        inverse = dinv[...]
        inv_ref[pl.ds(at, BLOCK), :] = inverse
        hi, lo = split(inverse)
        inverse = jnp.concatenate([hi, lo, hi], axis=1)
        for i in range(blocks):
            rows = slice(i * BLOCK, (i + 1) * BLOCK)
            hi, lo = split(work[rows, pl.ds(at, BLOCK)])
            new = dot_t(jnp.concatenate([hi, hi, lo], axis=1), inverse)
            new = jnp.where(i > k, new, 0.0)
            low_ref[rows, pl.ds(at, BLOCK)] = new
            hi, lo = split(new)
            left_ref[rows, :] = jnp.concatenate([hi, hi, lo], axis=1)
            right_ref[rows, :] = jnp.concatenate([hi, lo, hi], axis=1)
        ahead = right_ref[pl.ds(after, BLOCK), :]
        for i in range(blocks):
            rows = slice(i * BLOCK, (i + 1) * BLOCK)
            work[rows, pl.ds(after, BLOCK)] = work[rows, pl.ds(after, BLOCK)] - dot_t(left_ref[rows, :], ahead)
        right_ref[pl.ds(after, BLOCK), :] = jnp.zeros_like(ahead)
        return 0

    lax.fori_loop(0, blocks, step, 0)


def cholesky_parts(where, mine, other):
    count, strip, packed = mine.shape
    width = 4 * count * strip
    vmem = pl.BlockSpec(memory_space=pltpu.VMEM)
    return pl.pallas_call(
        chol_kernel,
        out_shape=(
            jax.ShapeDtypeStruct((width, width), jnp.float32),
            jax.ShapeDtypeStruct((width, BLOCK), jnp.float32),
        ),
        in_specs=[pl.BlockSpec(memory_space=pltpu.SMEM), vmem, vmem],
        out_specs=(vmem, vmem),
        scratch_shapes=[
            pltpu.VMEM((width, width), jnp.float32),
            pltpu.VMEM((2 * count, strip, packed), jnp.float32),
            pltpu.VMEM((BLOCK, BLOCK), jnp.float32),
            pltpu.VMEM((BLOCK, BLOCK), jnp.float32),
            pltpu.VMEM((width, 3 * BLOCK), jnp.bfloat16),
            pltpu.VMEM((width, 3 * BLOCK), jnp.bfloat16),
            pltpu.VMEM((8 * SUB * SUB, BLOCK), jnp.float32),
            pltpu.VMEM((BLOCK, BLOCK), jnp.float32),
        ],
        compiler_params=pltpu.CompilerParams(vmem_limit_bytes=32 << 20),
        cost_estimate=pl.CostEstimate(flops=80_000_000_000, bytes_accessed=8 << 20, transcendentals=0),
    )(where, mine, other)


def solve_kernel(gram_ref, low_ref, inv_ref, out_ref):
    _, width = gram_ref.shape
    blocks = width // BLOCK
    out_ref[...] = gram_ref[...]
    for k in range(blocks):
        cols = slice(k * BLOCK, (k + 1) * BLOCK)
        new = dot3_t(split(out_ref[:, cols]), split(inv_ref[cols, :]))
        out_ref[:, cols] = new
        if k + 1 < blocks:
            rest = slice((k + 1) * BLOCK, width)
            out_ref[:, rest] = out_ref[:, rest] - dot3_t(split(new), split(low_ref[rest, cols]))


def solve_rows(gram, low, inv):
    return pl.pallas_call(
        solve_kernel,
        out_shape=jax.ShapeDtypeStruct(gram.shape, jnp.float32),
        in_specs=[pl.BlockSpec(memory_space=pltpu.VMEM)] * 3,
        out_specs=pl.BlockSpec(memory_space=pltpu.VMEM),
        compiler_params=pltpu.CompilerParams(vmem_limit_bytes=24 << 20),
    )(gram, low, inv)


BOTH = ("obs", "unk")
OBS, UNK = 8, 16
CHIPS = UNK // 2
LINE = 4
STRIPS = 2 * LINE
WIDTH = 1024


def add_all(parts):
    total = parts[0]
    for part in parts[1:]:
        total = total + part
    return total


def swap_cores(value):
    return lax.ppermute(value, "unk", [(u, u ^ 1) for u in range(UNK)])


def over_chips(value, chips):
    got = [value]
    for k in range(1, chips):
        got.append(lax.ppermute(value, "unk", [(u, u ^ (2 * k)) for u in range(UNK)]))
    return got


def from_distance(value, k):
    return lax.ppermute(value, "obs", [(o, o ^ k) for o in range(OBS)])


def high_dot(left, right):
    return lax.dot_general(
        left, right, (((0,), (0,)), ((), ())),
        precision=lax.Precision.HIGH, preferred_element_type=jnp.float32,
    )


def local(design, weights):
    obs, unk = lax.axis_index("obs"), lax.axis_index("unk")
    chip, core = unk // 2, unk % 2
    rows = design.shape[0] // 2

    chunk = jnp.where(unk == 0, design[:, :BLOCK], 0.0)
    for j in range(1, CHIPS):
        pairs = [(o * UNK, o * UNK + 2 * j) for o in range(OBS)]
        chunk = chunk + lax.ppermute(design[:, j * BLOCK : (j + 1) * BLOCK], BOTH, pairs)

    def core_half(half):
        cut = lambda values: lax.dynamic_slice_in_dim(values, half * rows, rows, 0)
        return cut(design) * cut(weights)[:, None]

    chunk, first, second = lax.optimization_barrier((chunk, core_half(core), core_half(1 - core)))
    lower = swap_cores(chunk[rows:])
    part = jnp.where(core == 0, chunk[:rows], lower)
    mine = jnp.zeros((rows, WIDTH), jnp.float32)
    columns = over_chips(part, CHIPS)
    for k, got in enumerate(columns):
        mine = lax.dynamic_update_slice(mine, got, (0, (chip ^ k) * BLOCK))
    other = swap_cores(mine)
    first_weights = lax.dynamic_slice_in_dim(weights, core * rows, rows, 0)[:, None]
    second_weights = lax.dynamic_slice_in_dim(weights, (1 - core) * rows, rows, 0)[:, None]

    spot = chip % LINE * 2 + core

    def strips(values, scale):
        low = lax.dynamic_slice_in_dim(values, spot * STRIP, STRIP, 1)
        high = lax.dynamic_slice_in_dim(values, (2 * STRIPS - 1 - spot) * STRIP, STRIP, 1)
        return jnp.concatenate([low, high], axis=1) * scale

    strip = high_dot(strips(mine, first_weights), mine)
    partial_value = high_dot(first, mine)
    strip, partial_value, other = lax.optimization_barrier((strip, partial_value, other))
    strip = strip + high_dot(strips(other, second_weights), other)
    cut = (spot * STRIP // BLOCK + 1) * BLOCK
    high = jnp.pad(strip[STRIP:], ((0, 0), (WIDTH, BLOCK)))
    high = lax.dynamic_slice_in_dim(high, WIDTH - cut, WIDTH + BLOCK, 1)
    lanes = lax.broadcasted_iota(jnp.int32, high.shape, 1)
    piece = jnp.where(lanes < cut, jnp.pad(strip[:STRIP], ((0, 0), (0, BLOCK))), high)
    piece, partial_value, other = lax.optimization_barrier((piece, partial_value, other))
    came = from_distance(piece, 4)
    partial_value = partial_value + high_dot(second, other)
    piece, partial_value = lax.optimization_barrier((piece + came, partial_value))
    came = from_distance(piece, 1)
    owned = partial_value.shape[0] // OBS
    sends = [lax.dynamic_slice_in_dim(partial_value, (obs ^ k) * owned, owned, 0) for k in range(OBS)]
    piece, sends = lax.optimization_barrier((piece + came, sends))
    came = from_distance(piece, 2)
    piece = piece + came
    received = []
    for k in range(1, OBS):
        received.append(from_distance(sends[k], k))
    gathered = over_chips(piece, LINE)
    mine_top = jnp.stack(gathered)
    other_top = swap_cores(mine_top)
    where = jnp.stack([chip % LINE, core]).astype(jnp.int32)
    low, inverse = cholesky_parts(where, mine_top, other_top)
    owned_rows = add_all([sends[0]] + received)
    return solve_rows(owned_rows, low, inverse)


def solution(mesh):
    return jax.shard_map(
        local,
        mesh=mesh,
        in_specs=(P("obs", "unk"), P("obs")),
        out_specs=P(("unk", "obs"), None),
        check_vma=False,
    )
```

profile of v0, /device:TPU:7, one launch (start us, length us, event | category | flops | bytes accessed | tf_op | source)
XLA Modules:
  0.0 245.3 jit_solution(6805651883963277758)
XLA Ops:
  0.0 3.1 %fusion.11 = (f32[1024,128]{1,0:T(8,128)S(1)}, f32[1024,128]{1,0:T(8,128)}, f32[1024,128]{1,0:T(8,128)S(1)}, f32[1024,128]{1,0:T(8,128)S(1)}, f32[1024,128]{1,0:...) fusion(f32[1024,1536]{1,0:T(8,128)} %param.2), kind=kLoop, calls=%fused_computation.43 | loop fusion | bytes 7340032 | tf_op jit(solution)/shard_map/slice | solution.py:231
  12.0 5.9 %dynamic-slice_multiply_fusion = (f32[512,1536]{1,0:T(8,128)}, f32[512,1536]{1,0:T(8,128)}) fusion(f32[1024,1536]{1,0:T(8,128)} %param.2, s32[]{:T(128)S(6)} %select_n.117, f32[512]{0:T(512)S(1)} %get-tuple-element.74, f32[512]{0:T(512)S(1)} %get-tuple-element.75, s32[]{:T(128)S(6)} %select_n.116), kind=kLoop, calls=%fused_computation.1 | loop fusion | flops 1572864 | bytes 12587016 | tf_op jit(solution)/shard_map/mul | solution.py:235
  17.9 2.1 add_add_fusion.1
  20.1 8.1 %collective-permute-start.7 = (f32[512,128]{1,0:T(8,128)S(1)}, f32[512,128]{1,0:T(8,128)S(1)}, u32[]{:S(2)}, u32[]{:S(2)}) collective-permute-start(f32[512,128]{1,0:T(8,128)S(1)} %slice.45), channel_id=1, source_target_pairs={{0,1},{1,0},{2,3},{3,2},{4,5},{5,4},{6,7},{7,6},{8,9},{9,8},{10,11... | collective-permute-start | bytes 786440 | tf_op jit(solution)/shard_map/ppermute | solution.py:202
  29.6 5.4 %collective-permute-start.8 = (f32[512,128]{1,0:T(8,128)S(1)}, f32[512,128]{1,0:T(8,128)S(1)}, u32[]{:S(2)}, u32[]{:S(2)}) collective-permute-start(f32[512,128]{1,0:T(8,128)S(1)} %get-tuple-element.50), channel_id=1, source_target_pairs={{0,2},{1,3},{2,0},{3,1},{4,6},{5,7},{6,4},{7,5},{8,10},{9,11},{10,... | collective-permute-start | bytes 786440 | tf_op jit(solution)/shard_map/ppermute | solution.py:208
  35.1 6.3 %collective-permute-start.9 = (f32[512,128]{1,0:T(8,128)S(1)}, f32[512,128]{1,0:T(8,128)S(1)}, u32[]{:S(2)}, u32[]{:S(2)}) collective-permute-start(f32[512,128]{1,0:T(8,128)S(1)} %get-tuple-element.50), channel_id=1, source_target_pairs={{0,4},{1,5},{2,6},{3,7},{4,0},{5,1},{6,2},{7,3},{8,12},{9,13},{10,... | collective-permute-start | bytes 786440 | tf_op jit(solution)/shard_map/ppermute | solution.py:208
  41.6 1.8 collective-permute-start.12
  43.4 2.8 %collective-permute-start.13 = (f32[512,128]{1,0:T(8,128)S(1)}, f32[512,128]{1,0:T(8,128)S(1)}, u32[]{:S(2)}, u32[]{:S(2)}) collective-permute-start(f32[512,128]{1,0:T(8,128)S(1)} %get-tuple-element.50), channel_id=1, source_target_pairs={{0,12},{1,13},{2,14},{3,15},{4,8},{5,9},{6,10},{7,11},{8,4},{9,5},... | collective-permute-start | bytes 786440 | tf_op jit(solution)/shard_map/ppermute | solution.py:208
  46.2 7.1 %collective-permute-done.9 = f32[512,128]{1,0:T(8,128)S(1)} collective-permute-done((f32[512,128]{1,0:T(8,128)S(1)}, f32[512,128]{1,0:T(8,128)S(1)}, u32[]{:S(2)}, u32[]{:S(2)}) %collective-permute-start.9) | collective-permute-done | bytes 262176 | tf_op jit(solution)/shard_map/ppermute | solution.py:208
  53.3 2.1 collective-permute-done.10
  55.5 10.3 %collective-permute-done.11 = f32[512,128]{1,0:T(8,128)S(1)} collective-permute-done((f32[512,128]{1,0:T(8,128)S(1)}, f32[512,128]{1,0:T(8,128)S(1)}, u32[]{:S(2)}, u32[]{:S(2)}) %collective-permute-start.11) | collective-permute-done | bytes 262176 | tf_op jit(solution)/shard_map/ppermute | solution.py:208
  70.1 5.6 %fusion.14 = f32[1536,1024]{1,0:T(8,128)S(1)} fusion(f32[512,1536]{1,0:T(8,128)S(1)} %copy-done, f32[512,1024]{1,0:T(8,128)S(1)} %constant_dynamic-update-slice_fusion), kind=kOutput, calls=%fused_computation.46 | convolution fusion | flops 4831838208 | bytes 11534336 | tf_op jit(solution)/shard_map/dot_general | solution.py:217
  77.0 2.5 %fusion.4 = f32[128,1024]{1,0:T(8,128)S(1)} fusion(f32[512,1024]{1,0:T(8,128)} %collective-permute-done.15, f32[512,64]{1,0:T(8,128)S(1)} %get-tuple-element.69, f32[512,64]{1,0:T(8,128)S(1)} %get-tuple-element.68, f32[512]{0:T(512)S(1)} %get-tuple-element.74), kind=kOutput, calls=%fused_computation.13 | convolution fusion | flops 402784256 | bytes 2885632 | tf_op jit(solution)/shard_map/dot_general | solution.py:217
  79.7 3.4 %collective-permute-start.16 = (f32[64,1152]{1,0:T(8,128)S(1)}, f32[64,1152]{1,0:T(8,128)S(1)}, u32[]{:S(2)}, u32[]{:S(2)}) collective-permute-start(f32[64,1152]{1,0:T(8,128)S(1)} %fusion), channel_id=1, source_target_pairs={{0,64},{16,80},{32,96},{48,112},{64,0},{80,16},{96,32},{112,48},{1... | collective-permute-start | bytes 884744 | tf_op jit(solution)/shard_map/ppermute | solution.py:213
  83.1 9.1 %convolution_add_fusion = f32[1536,1024]{1,0:T(8,128)} fusion(f32[1536,1024]{1,0:T(8,128)S(1)} %fusion.14, f32[512,1536]{1,0:T(8,128)S(1)} %copy-done.1, f32[512,1024]{1,0:T(8,128)} %collective-permute-done.15), kind=kOutput, calls=%fused_computation | convolution fusion | flops 4833411072 | bytes 17825792 | tf_op jit(solution)/shard_map/dot_general | solution.py:217
  93.6 3.6 %constant_dynamic-slice_fusion = (f32[192,1024]{1,0:T(8,128)S(1)}, f32[192,1024]{1,0:T(8,128)S(1)}, f32[192,1024]{1,0:T(8,128)S(1)}, f32[192,1024]{1,0:T(8,128)S...) fusion(f32[1536,1024]{1,0:T(8,128)} %convolution_add_fusion, ...), kind=kLoop, calls=%fused_computation.20 | loop fusion | bytes 12582944 | tf_op jit(solution)/shard_map/dynamic_slice | solution.py:270
  97.2 3.3 %collective-permute-done.17 = f32[64,1152]{1,0:T(8,128)S(1)} collective-permute-done((f32[64,1152]{1,0:T(8,128)S(1)}, f32[64,1152]{1,0:T(8,128)S(1)}, u32[]{:S(2)}, u32[]{:S(2)}) %collective-permute-start.17) | collective-permute-done | bytes 294944 | tf_op jit(solution)/shard_map/ppermute | solution.py:213
  100.5 3.0 %collective-permute-start.25 = (f32[64,1152]{1,0:T(8,128)S(1)}, f32[64,1152]{1,0:T(8,128)S(1)}, u32[]{:S(2)}, u32[]{:S(2)}) collective-permute-start(f32[64,1152]{1,0:T(8,128)S(1)} %add.174), channel_id=1, source_target_pairs={{0,32},{16,48},{32,0},{48,16},{64,96},{80,112},{96,64},{112,80},{1... | collective-permute-start | bytes 884744 | tf_op jit(solution)/shard_map/ppermute | solution.py:213
  103.5 2.3 collective-permute-start.24
  105.8 2.3 collective-permute-start.23
  109.5 2.7 %collective-permute-start.28 = (f32[64,1152]{1,0:T(8,128)S(1)}, f32[64,1152]{1,0:T(8,128)S(1)}, u32[]{:S(2)}, u32[]{:S(2)}) collective-permute-start(f32[64,1152]{1,0:T(8,128)S(1)} %add.190), channel_id=1, source_target_pairs={{0,6},{1,7},{2,4},{3,5},{4,2},{5,3},{6,0},{7,1},{8,14},{9,15},{10,... | collective-permute-start | bytes 884744 | tf_op jit(solution)/shard_map/ppermute | solution.py:208
  112.2 3.0 %collective-permute-start.22 = (f32[192,1024]{1,0:T(8,128)S(1)}, f32[192,1024]{1,0:T(8,128)S(1)}, u32[]{:S(2)}, u32[]{:S(2)}) collective-permute-start(f32[192,1024]{1,0:T(8,128)S(1)} %get-tuple-element.43), channel_id=1, source_target_pairs={{0,80},{16,64},{32,112},{48,96},{64,16},{80,0},{96,48},{112,32},{1... | collective-permute-start | bytes 2359304 | tf_op jit(solution)/shard_map/ppermute | solution.py:213
  117.5 5.2 %collective-permute-done.27 = f32[64,1152]{1,0:T(8,128)S(1)} collective-permute-done((f32[64,1152]{1,0:T(8,128)S(1)}, f32[64,1152]{1,0:T(8,128)S(1)}, u32[]{:S(2)}, u32[]{:S(2)}) %collective-permute-start.27) | collective-permute-done | bytes 294944 | tf_op jit(solution)/shard_map/ppermute | solution.py:208
  123.7 1.7 collective-permute-done.26
  125.4 4.4 %collective-permute-start.20 = (f32[192,1024]{1,0:T(8,128)S(1)}, f32[192,1024]{1,0:T(8,128)S(1)}, u32[]{:S(2)}, u32[]{:S(2)}) collective-permute-start(f32[192,1024]{1,0:T(8,128)S(1)} %get-tuple-element.41), channel_id=1, source_target_pairs={{0,48},{16,32},{32,16},{48,0},{64,112},{80,96},{96,80},{112,64},{1... | collective-permute-start | bytes 2359304 | tf_op jit(solution)/shard_map/ppermute | solution.py:213
  129.8 27.6 %collective-permute-done.24 = f32[192,1024]{1,0:T(8,128)S(1)} collective-permute-done((f32[192,1024]{1,0:T(8,128)S(1)}, f32[192,1024]{1,0:T(8,128)S(1)}, u32[]{:S(2)}, u32[]{:S(2)}) %collective-permute-start.24) | collective-permute-done | bytes 786464 | tf_op jit(solution)/shard_map/ppermute | solution.py:213
  157.4 7.6 %collective-permute-start.19 = (f32[192,1024]{1,0:T(8,128)S(1)}, f32[192,1024]{1,0:T(8,128)S(1)}, u32[]{:S(2)}, u32[]{:S(2)}) collective-permute-start(f32[192,1024]{1,0:T(8,128)S(1)} %get-tuple-element.40), channel_id=1, source_target_pairs={{0,32},{16,48},{32,0},{48,16},{64,96},{80,112},{96,64},{112,80},{1... | collective-permute-start | bytes 2359304 | tf_op jit(solution)/shard_map/ppermute | solution.py:213
  166.9 13.1 %collective-permute-done.21 = f32[192,1024]{1,0:T(8,128)S(1)} collective-permute-done((f32[192,1024]{1,0:T(8,128)S(1)}, f32[192,1024]{1,0:T(8,128)S(1)}, u32[]{:S(2)}, u32[]{:S(2)}) %collective-permute-start.21) | collective-permute-done | bytes 786464 | tf_op jit(solution)/shard_map/ppermute | solution.py:213
  180.0 10.0 %collective-permute-done.20 = f32[192,1024]{1,0:T(8,128)S(1)} collective-permute-done((f32[192,1024]{1,0:T(8,128)S(1)}, f32[192,1024]{1,0:T(8,128)S(1)}, u32[]{:S(2)}, u32[]{:S(2)}) %collective-permute-start.20) | collective-permute-done | bytes 786464 | tf_op jit(solution)/shard_map/ppermute | solution.py:213
  190.0 8.0 %collective-permute-done.18 = f32[192,1024]{1,0:T(8,128)S(1)} collective-permute-done((f32[192,1024]{1,0:T(8,128)S(1)}, f32[192,1024]{1,0:T(8,128)S(1)}, u32[]{:S(2)}, u32[]{:S(2)}) %collective-permute-start.18) | collective-permute-done | bytes 786464 | tf_op jit(solution)/shard_map/ppermute | solution.py:213
  198.6 42.1 %shard_map.28 = (f32[1024,1024]{1,0:T(8,128)S(1)}, f32[1024,128]{1,0:T(8,128)S(1)}) custom-call(s32[2]{0:T(128)S(1)} %pad_add_fusion.where_ref, f32[4,64,1152]{2,1,0:T(8,128)S(1)} %pad_maximum_fusion.mine_ref, f32[4,64,1152]{2,1,0:T(8,128)S(1)} %collective-permute-done.29.other_ref), custom_call_target="tpu_custom_call" | custom-call | flops 80000000000 | bytes 8388608 | tf_op jit(solution)/shard_map/pallas_call | solution.py:140
  240.8 4.6 %shard_map.29 = f32[192,1024]{1,0:T(8,128)} custom-call(f32[192,1024]{1,0:T(8,128)S(1)} %add_add_fusion.gram_ref, f32[1024,1024]{1,0:T(8,128)S(1)} %get-tuple-element.47.low_ref, f32[1024,128]{1,0:T(8,128)S(1)} %get-tuple-element.48.inv_ref), custom_call_target="tpu_custom_call" | custom-call | tf_op jit(solution)/shard_map/pallas_call | solution.py:177
  (67 shorter events, 24.9 us)
Async XLA Ops:
  0.0 10.5 %copy-start.2 = (f32[1024]{0:T(1024)S(1)}, f32[1024]{0:T(1024)}, u32[]{:S(2)}) copy-start(f32[1024]{0:T(1024)} %param.3) | copy-start | bytes 12292
  3.1 7.5 %collective-permute-start.6 = (f32[1024,128]{1,0:T(8,128)}, f32[1024,128]{1,0:T(8,128)}, u32[]{:S(2)}, u32[]{:S(2)}) collective-permute-start(f32[1024,128]{1,0:T(8,128)} %get-tuple-element.62), channel_id=1, source_target_pairs={{0,14},{16,30},{32,46},{48,62},{64,78},{80,94},{96,110},{112,126}} | collective-permute-start | bytes 1572872 | tf_op jit(solution)/shard_map/ppermute | solution.py:231
  4.6 6.7 %collective-permute-start.5 = (f32[1024,128]{1,0:T(8,128)S(1)}, f32[1024,128]{1,0:T(8,128)}, u32[]{:S(2)}, u32[]{:S(2)}) collective-permute-start(f32[1024,128]{1,0:T(8,128)S(1)} %get-tuple-element.63), channel_id=1, source_target_pairs={{0,12},{16,28},{32,44},{48,60},{64,76},{80,92},{96,108},{112,124}} | collective-permute-start | bytes 1572872 | tf_op jit(solution)/shard_map/ppermute | solution.py:231
  6.0 11.9 %collective-permute-start.4 = (f32[1024,128]{1,0:T(8,128)S(1)}, f32[1024,128]{1,0:T(8,128)}, u32[]{:S(2)}, u32[]{:S(2)}) collective-permute-start(f32[1024,128]{1,0:T(8,128)S(1)} %get-tuple-element.64), channel_id=1, source_target_pairs={{0,10},{16,26},{32,42},{48,58},{64,74},{80,90},{96,106},{112,122}} | collective-permute-start | bytes 1572872 | tf_op jit(solution)/shard_map/ppermute | solution.py:231
  7.5 10.4 %collective-permute-start.3 = (f32[1024,128]{1,0:T(8,128)S(1)}, f32[1024,128]{1,0:T(8,128)}, u32[]{:S(2)}, u32[]{:S(2)}) collective-permute-start(f32[1024,128]{1,0:T(8,128)S(1)} %get-tuple-element.65), channel_id=1, source_target_pairs={{0,8},{16,24},{32,40},{48,56},{64,72},{80,88},{96,104},{112,120}} | collective-permute-start | bytes 1572872 | tf_op jit(solution)/shard_map/ppermute | solution.py:231
  9.0 8.9 %collective-permute-start.2 = (f32[1024,128]{1,0:T(8,128)S(1)}, f32[1024,128]{1,0:T(8,128)}, u32[]{:S(2)}, u32[]{:S(2)}) collective-permute-start(f32[1024,128]{1,0:T(8,128)S(1)} %get-tuple-element.66), channel_id=1, source_target_pairs={{0,6},{16,22},{32,38},{48,54},{64,70},{80,86},{96,102},{112,118}} | collective-permute-start | bytes 1572872 | tf_op jit(solution)/shard_map/ppermute | solution.py:231
  10.6 7.3 %collective-permute-start.1 = (f32[1024,128]{1,0:T(8,128)S(1)}, f32[1024,128]{1,0:T(8,128)S(1)}, u32[]{:S(2)}, u32[]{:S(2)}) collective-permute-start(f32[1024,128]{1,0:T(8,128)S(1)} %get-tuple-element.67), channel_id=1, source_target_pairs={{0,4},{16,20},{32,36},{48,52},{64,68},{80,84},{96,100},{112,116}} | collective-permute-start | bytes 1572872 | tf_op jit(solution)/shard_map/ppermute | solution.py:231
  11.3 6.6 %collective-permute-start = (f32[1024,128]{1,0:T(8,128)S(1)}, f32[1024,128]{1,0:T(8,128)S(1)}, u32[]{:S(2)}, u32[]{:S(2)}) collective-permute-start(f32[1024,128]{1,0:T(8,128)S(1)} %get-tuple-element.61), channel_id=1, source_target_pairs={{0,2},{16,18},{32,34},{48,50},{64,66},{80,82},{96,98},{112,114}} | collective-permute-start | bytes 1572872 | tf_op jit(solution)/shard_map/ppermute | solution.py:231
  20.1 9.3 %collective-permute-start.7 = (f32[512,128]{1,0:T(8,128)S(1)}, f32[512,128]{1,0:T(8,128)S(1)}, u32[]{:S(2)}, u32[]{:S(2)}) collective-permute-start(f32[512,128]{1,0:T(8,128)S(1)} %slice.45), channel_id=1, source_target_pairs={{0,1},{1,0},{2,3},{3,2},{4,5},{5,4},{6,7},{7,6},{8,9},{9,8},{10,11... | collective-permute-start | bytes 786440 | tf_op jit(solution)/shard_map/ppermute | solution.py:202
  29.6 13.7 %collective-permute-start.8 = (f32[512,128]{1,0:T(8,128)S(1)}, f32[512,128]{1,0:T(8,128)S(1)}, u32[]{:S(2)}, u32[]{:S(2)}) collective-permute-start(f32[512,128]{1,0:T(8,128)S(1)} %get-tuple-element.50), channel_id=1, source_target_pairs={{0,2},{1,3},{2,0},{3,1},{4,6},{5,7},{6,4},{7,5},{8,10},{9,11},{10,... | collective-permute-start | bytes 786440 | tf_op jit(solution)/shard_map/ppermute | solution.py:208
  35.1 18.2 %collective-permute-start.9 = (f32[512,128]{1,0:T(8,128)S(1)}, f32[512,128]{1,0:T(8,128)S(1)}, u32[]{:S(2)}, u32[]{:S(2)}) collective-permute-start(f32[512,128]{1,0:T(8,128)S(1)} %get-tuple-element.50), channel_id=1, source_target_pairs={{0,4},{1,5},{2,6},{3,7},{4,0},{5,1},{6,2},{7,3},{8,12},{9,13},{10,... | collective-permute-start | bytes 786440 | tf_op jit(solution)/shard_map/ppermute | solution.py:208
  41.4 14.0 %collective-permute-start.10 = (f32[512,128]{1,0:T(8,128)S(1)}, f32[512,128]{1,0:T(8,128)S(1)}, u32[]{:S(2)}, u32[]{:S(2)}) collective-permute-start(f32[512,128]{1,0:T(8,128)S(1)} %get-tuple-element.50), channel_id=1, source_target_pairs={{0,6},{1,7},{2,4},{3,5},{4,2},{5,3},{6,0},{7,1},{8,14},{9,15},{10,... | collective-permute-start | bytes 786440 | tf_op jit(solution)/shard_map/ppermute | solution.py:208
  41.6 24.2 %collective-permute-start.11 = (f32[512,128]{1,0:T(8,128)S(1)}, f32[512,128]{1,0:T(8,128)S(1)}, u32[]{:S(2)}, u32[]{:S(2)}) collective-permute-start(f32[512,128]{1,0:T(8,128)S(1)} %get-tuple-element.50), channel_id=1, source_target_pairs={{0,8},{1,9},{2,10},{3,11},{4,12},{5,13},{6,14},{7,15},{8,0},{9,1},... | collective-permute-start | bytes 786440 | tf_op jit(solution)/shard_map/ppermute | solution.py:208
  41.6 24.2 %collective-permute-start.12 = (f32[512,128]{1,0:T(8,128)S(1)}, f32[512,128]{1,0:T(8,128)S(1)}, u32[]{:S(2)}, u32[]{:S(2)}) collective-permute-start(f32[512,128]{1,0:T(8,128)S(1)} %get-tuple-element.50), channel_id=1, source_target_pairs={{0,10},{1,11},{2,8},{3,9},{4,14},{5,15},{6,12},{7,13},{8,2},{9,3},... | collective-permute-start | bytes 786440 | tf_op jit(solution)/shard_map/ppermute | solution.py:208
  43.4 22.5 %collective-permute-start.13 = (f32[512,128]{1,0:T(8,128)S(1)}, f32[512,128]{1,0:T(8,128)S(1)}, u32[]{:S(2)}, u32[]{:S(2)}) collective-permute-start(f32[512,128]{1,0:T(8,128)S(1)} %get-tuple-element.50), channel_id=1, source_target_pairs={{0,12},{1,13},{2,14},{3,15},{4,8},{5,9},{6,10},{7,11},{8,4},{9,5},... | collective-permute-start | bytes 786440 | tf_op jit(solution)/shard_map/ppermute | solution.py:208
  53.3 13.8 %collective-permute-start.14 = (f32[512,128]{1,0:T(8,128)S(1)}, f32[512,128]{1,0:T(8,128)S(1)}, u32[]{:S(2)}, u32[]{:S(2)}) collective-permute-start(f32[512,128]{1,0:T(8,128)S(1)} %get-tuple-element.50), channel_id=1, source_target_pairs={{0,14},{1,15},{2,12},{3,13},{4,10},{5,11},{6,8},{7,9},{8,6},{9,7},... | collective-permute-start | bytes 786440 | tf_op jit(solution)/shard_map/ppermute | solution.py:208
  67.1 8.6 %collective-permute-start.15 = (f32[512,1024]{1,0:T(8,128)S(1)}, f32[512,1024]{1,0:T(8,128)}, u32[]{:S(2)}, u32[]{:S(2)}) collective-permute-start(f32[512,1024]{1,0:T(8,128)S(1)} %constant_dynamic-update-slice_fusion), channel_id=1, source_target_pairs={{0,1},{1,0},{2,3},{3,2},{4,5},{5,4},{6,7},{7,6},{8,9},{9,8},{10,11... | collective-permute-start | bytes 6291464 | tf_op jit(solution)/shard_map/ppermute | solution.py:202
  79.5 3.6 %copy-start.1 = (f32[512,1536]{1,0:T(8,128)S(1)}, f32[512,1536]{1,0:T(8,128)}, u32[]{:S(2)}) copy-start(f32[512,1536]{1,0:T(8,128)} %get-tuple-element.34) | copy-start | bytes 9437188
  79.7 12.5 %collective-permute-start.16 = (f32[64,1152]{1,0:T(8,128)S(1)}, f32[64,1152]{1,0:T(8,128)S(1)}, u32[]{:S(2)}, u32[]{:S(2)}) collective-permute-start(f32[64,1152]{1,0:T(8,128)S(1)} %fusion), channel_id=1, source_target_pairs={{0,64},{16,80},{32,96},{48,112},{64,0},{80,16},{96,32},{112,48},{1... | collective-permute-start | bytes 884744 | tf_op jit(solution)/shard_map/ppermute | solution.py:213
  92.2 8.3 %collective-permute-start.17 = (f32[64,1152]{1,0:T(8,128)S(1)}, f32[64,1152]{1,0:T(8,128)S(1)}, u32[]{:S(2)}, u32[]{:S(2)}) collective-permute-start(f32[64,1152]{1,0:T(8,128)S(1)} %add.172), channel_id=1, source_target_pairs={{0,16},{16,0},{32,48},{48,32},{64,80},{80,64},{96,112},{112,96},{1... | collective-permute-start | bytes 884744 | tf_op jit(solution)/shard_map/ppermute | solution.py:213
  100.5 8.9 %collective-permute-start.25 = (f32[64,1152]{1,0:T(8,128)S(1)}, f32[64,1152]{1,0:T(8,128)S(1)}, u32[]{:S(2)}, u32[]{:S(2)}) collective-permute-start(f32[64,1152]{1,0:T(8,128)S(1)} %add.174), channel_id=1, source_target_pairs={{0,32},{16,48},{32,0},{48,16},{64,96},{80,112},{96,64},{112,80},{1... | collective-permute-start | bytes 884744 | tf_op jit(solution)/shard_map/ppermute | solution.py:213
  103.5 53.9 %collective-permute-start.24 = (f32[192,1024]{1,0:T(8,128)S(1)}, f32[192,1024]{1,0:T(8,128)S(1)}, u32[]{:S(2)}, u32[]{:S(2)}) collective-permute-start(f32[192,1024]{1,0:T(8,128)S(1)} %get-tuple-element.45), channel_id=1, source_target_pairs={{0,112},{16,96},{32,80},{48,64},{64,48},{80,32},{96,16},{112,0},{1... | collective-permute-start | bytes 2359304 | tf_op jit(solution)/shard_map/ppermute | solution.py:213
  105.8 59.2 %collective-permute-start.23 = (f32[192,1024]{1,0:T(8,128)S(1)}, f32[192,1024]{1,0:T(8,128)S(1)}, u32[]{:S(2)}, u32[]{:S(2)}) collective-permute-start(f32[192,1024]{1,0:T(8,128)S(1)} %get-tuple-element.44), channel_id=1, source_target_pairs={{0,96},{16,112},{32,64},{48,80},{64,32},{80,48},{96,0},{112,16},{1... | collective-permute-start | bytes 2359304 | tf_op jit(solution)/shard_map/ppermute | solution.py:213
  109.5 7.2 %collective-permute-start.28 = (f32[64,1152]{1,0:T(8,128)S(1)}, f32[64,1152]{1,0:T(8,128)S(1)}, u32[]{:S(2)}, u32[]{:S(2)}) collective-permute-start(f32[64,1152]{1,0:T(8,128)S(1)} %add.190), channel_id=1, source_target_pairs={{0,6},{1,7},{2,4},{3,5},{4,2},{5,3},{6,0},{7,1},{8,14},{9,15},{10,... | collective-permute-start | bytes 884744 | tf_op jit(solution)/shard_map/ppermute | solution.py:208
  112.2 52.9 %collective-permute-start.22 = (f32[192,1024]{1,0:T(8,128)S(1)}, f32[192,1024]{1,0:T(8,128)S(1)}, u32[]{:S(2)}, u32[]{:S(2)}) collective-permute-start(f32[192,1024]{1,0:T(8,128)S(1)} %get-tuple-element.43), channel_id=1, source_target_pairs={{0,80},{16,64},{32,112},{48,96},{64,16},{80,0},{96,48},{112,32},{1... | collective-permute-start | bytes 2359304 | tf_op jit(solution)/shard_map/ppermute | solution.py:213
  115.2 7.4 %collective-permute-start.27 = (f32[64,1152]{1,0:T(8,128)S(1)}, f32[64,1152]{1,0:T(8,128)S(1)}, u32[]{:S(2)}, u32[]{:S(2)}) collective-permute-start(f32[64,1152]{1,0:T(8,128)S(1)} %add.190), channel_id=1, source_target_pairs={{0,4},{1,5},{2,6},{3,7},{4,0},{5,1},{6,2},{7,3},{8,12},{9,13},{10,... | collective-permute-start | bytes 884744 | tf_op jit(solution)/shard_map/ppermute | solution.py:208
  116.7 8.8 %collective-permute-start.26 = (f32[64,1152]{1,0:T(8,128)S(1)}, f32[64,1152]{1,0:T(8,128)S(1)}, u32[]{:S(2)}, u32[]{:S(2)}) collective-permute-start(f32[64,1152]{1,0:T(8,128)S(1)} %add.190), channel_id=1, source_target_pairs={{0,2},{1,3},{2,0},{3,1},{4,6},{5,7},{6,4},{7,5},{8,10},{9,11},{10,... | collective-permute-start | bytes 884744 | tf_op jit(solution)/shard_map/ppermute | solution.py:208
  122.7 57.3 %collective-permute-start.21 = (f32[192,1024]{1,0:T(8,128)S(1)}, f32[192,1024]{1,0:T(8,128)S(1)}, u32[]{:S(2)}, u32[]{:S(2)}) collective-permute-start(f32[192,1024]{1,0:T(8,128)S(1)} %get-tuple-element.42), channel_id=1, source_target_pairs={{0,64},{16,80},{32,96},{48,112},{64,0},{80,16},{96,32},{112,48},{1... | collective-permute-start | bytes 2359304 | tf_op jit(solution)/shard_map/ppermute | solution.py:213
  125.4 64.5 %collective-permute-start.20 = (f32[192,1024]{1,0:T(8,128)S(1)}, f32[192,1024]{1,0:T(8,128)S(1)}, u32[]{:S(2)}, u32[]{:S(2)}) collective-permute-start(f32[192,1024]{1,0:T(8,128)S(1)} %get-tuple-element.41), channel_id=1, source_target_pairs={{0,48},{16,32},{32,16},{48,0},{64,112},{80,96},{96,80},{112,64},{1... | collective-permute-start | bytes 2359304 | tf_op jit(solution)/shard_map/ppermute | solution.py:213
  157.4 32.5 %collective-permute-start.19 = (f32[192,1024]{1,0:T(8,128)S(1)}, f32[192,1024]{1,0:T(8,128)S(1)}, u32[]{:S(2)}, u32[]{:S(2)}) collective-permute-start(f32[192,1024]{1,0:T(8,128)S(1)} %get-tuple-element.40), channel_id=1, source_target_pairs={{0,32},{16,48},{32,0},{48,16},{64,96},{80,112},{96,64},{112,80},{1... | collective-permute-start | bytes 2359304 | tf_op jit(solution)/shard_map/ppermute | solution.py:213
  165.0 32.9 %collective-permute-start.18 = (f32[192,1024]{1,0:T(8,128)S(1)}, f32[192,1024]{1,0:T(8,128)S(1)}, u32[]{:S(2)}, u32[]{:S(2)}) collective-permute-start(f32[192,1024]{1,0:T(8,128)S(1)} %get-tuple-element.39), channel_id=1, source_target_pairs={{0,16},{16,0},{32,48},{48,32},{64,80},{80,64},{96,112},{112,96},{1... | collective-permute-start | bytes 2359304 | tf_op jit(solution)/shard_map/ppermute | solution.py:213
  165.1 33.5 %collective-permute-start.29 = (f32[4,64,1152]{2,1,0:T(8,128)S(1)}, f32[4,64,1152]{2,1,0:T(8,128)S(1)}, u32[]{:S(2)}, u32[]{:S(2)}) collective-permute-start(f32[4,64,1152]{2,1,0:T(8,128)S(1)} %pad_maximum_fusion.mine_ref), channel_id=1, source_target_pairs={{0,1},{1,0},{2,3},{3,2},{4,5},{5,4},{6,7},{7,6},{8,9},{9,8},{10,11... | collective-permute-start | bytes 3538952 | tf_op jit(solution)/shard_map/ppermute | solution.py:202
  (1 other events, 1.9 us)
where the time goes:
time: 250 us; the launch traced here: 245 us
  waiting for transfers between devices  92.4 us (37%)
  starting transfers between devices  69.2 us (28%)
  Pallas kernels  46.7 us (19%)
  matrix products  18.2 us (7%)
  local copies, waits for them, and re-layouts  9.46 us (4%)
  other arithmetic  9.11 us (4%)
    ppermute x10, waiting for transfers between devices, from_distance(): return lax.ppermute(value, 'obs', [(o, o ^ k) for o in range(OBS)])  63.4 us
    pallas_call x1, Pallas kernels, cholesky_parts(): pl.pallas_call(chol_kernel, out_shape=(jax.ShapeDtypeStruct((width, width...  42.1 us
    ppermute x10, starting transfers between devices, from_distance(): return lax.ppermute(value, 'obs', [(o, o ^ k) for o in range(OBS)])  28.4 us
    ppermute x10, waiting for transfers between devices, over_chips(): got.append(lax.ppermute(value, 'unk', [(u, u ^ 2 * k) for u in range(UNK)]))  27.8 us
    ppermute x10, starting transfers between devices, over_chips(): got.append(lax.ppermute(value, 'unk', [(u, u ^ 2 * k) for u in range(UNK)]))  21.3 us
    dot_general x4, matrix products, high_dot(): lax.dot_general(left, right, (((0,), (0,)), ((), ())), precision=lax.Prec...  18.2 us
    ppermute x3, starting transfers between devices, swap_cores(): return lax.ppermute(value, 'unk', [(u, u ^ 1) for u in range(UNK)])  10.8 us
    ppermute x7, starting transfers between devices, local(): lax.ppermute(design[:, j * BLOCK:(j + 1) * BLOCK], BOTH, pairs)  8.77 us
  transfers between devices with their start and end apart: 30, of which 14 were waited for; matrix products, arithmetic and copies ran while one was open for 11% of the time, Pallas kernels for 0%

commit v1 on v0

--- a/solution.py
+++ b/solution.py
@@ -203,10 +203,9 @@
 
 
 def over_chips(value, chips):
-    got = [value]
-    for k in range(1, chips):
-        got.append(lax.ppermute(value, "unk", [(u, u ^ (2 * k)) for u in range(UNK)]))
-    return got
+    return [value] + [
+        lax.ppermute(value, "unk", [(u, u ^ (2 * k)) for u in range(UNK)]) for k in range(1, chips)
+    ]
 
 
 def from_distance(value, k):
@@ -238,8 +237,7 @@
     lower = swap_cores(chunk[rows:])
     part = jnp.where(core == 0, chunk[:rows], lower)
     mine = jnp.zeros((rows, WIDTH), jnp.float32)
-    columns = over_chips(part, CHIPS)
-    for k, got in enumerate(columns):
+    for k, got in enumerate(over_chips(part, CHIPS)):
         mine = lax.dynamic_update_slice(mine, got, (0, (chip ^ k) * BLOCK))
     other = swap_cores(mine)
     first_weights = lax.dynamic_slice_in_dim(weights, core * rows, rows, 0)[:, None]
@@ -253,19 +251,19 @@
         return jnp.concatenate([low, high], axis=1) * scale
 
     strip = high_dot(strips(mine, first_weights), mine)
-    partial_value = high_dot(first, mine)
-    strip, partial_value, other = lax.optimization_barrier((strip, partial_value, other))
+    strip, other = lax.optimization_barrier((strip, other))
     strip = strip + high_dot(strips(other, second_weights), other)
     cut = (spot * STRIP // BLOCK + 1) * BLOCK
     high = jnp.pad(strip[STRIP:], ((0, 0), (WIDTH, BLOCK)))
     high = lax.dynamic_slice_in_dim(high, WIDTH - cut, WIDTH + BLOCK, 1)
     lanes = lax.broadcasted_iota(jnp.int32, high.shape, 1)
     piece = jnp.where(lanes < cut, jnp.pad(strip[:STRIP], ((0, 0), (0, BLOCK))), high)
-    piece, partial_value, other = lax.optimization_barrier((piece, partial_value, other))
+    piece, mine, other = lax.optimization_barrier((piece, mine, other))
     came = from_distance(piece, 4)
+    partial_value = high_dot(first, mine)
+    piece, partial_value, other = lax.optimization_barrier((piece + came, partial_value, other))
+    came = from_distance(piece, 1)
     partial_value = partial_value + high_dot(second, other)
-    piece, partial_value = lax.optimization_barrier((piece + came, partial_value))
-    came = from_distance(piece, 1)
     owned = partial_value.shape[0] // OBS
     sends = [lax.dynamic_slice_in_dim(partial_value, (obs ^ k) * owned, owned, 0) for k in range(OBS)]
     piece, sends = lax.optimization_barrier((piece + came, sends))

time: 250 us -> 248 us (level)
  waiting for transfers between devices: 92.4 us -> 97.7 us
  starting transfers between devices: 69.2 us -> 64.8 us
  local copies, waits for them, and re-layouts: 9.46 us -> 5.69 us
  other arithmetic: 9.11 us -> 12.3 us
    ppermute x10, starting transfers between devices: 28.4 us -> 23.9 us  [from_distance(): return lax.ppermute(value, 'obs', [(o, o ^ k) for o in range(OBS)])]
    ppermute x10, waiting for transfers between devices: 63.4 us -> 66.4 us  [from_distance(): return lax.ppermute(value, 'obs', [(o, o ^ k) for o in range(OBS)])]
    dynamic_slice x1, local copies, waits for them, and re-layouts: 3.6 us -> 0.6 us  [local(): lax.dynamic_slice_in_dim(partial_value, (obs ^ k) * owned, owned, 0)]
    ppermute x3, waiting for transfers between devices: 1.17 us -> 3.95 us  [swap_cores(): return lax.ppermute(value, 'unk', [(u, u ^ 1) for u in range(UNK)])]
  transfers between devices with their start and end apart: 30 -> 30, of which waited for: 14 -> 15; matrix products, arithmetic and copies ran while one was open for 11% -> 10% of each run, Pallas kernels for 0% -> 0%
where the time goes in v1:
time: 248 us; the launch traced here: 243 us
  waiting for transfers between devices  97.7 us (39%)
  starting transfers between devices  64.8 us (26%)
  Pallas kernels  46.7 us (19%)
  matrix products  16 us (6%)
  other arithmetic  12.3 us (5%)
  local copies, waits for them, and re-layouts  5.69 us (2%)
    ppermute x10, waiting for transfers between devices, from_distance(): return lax.ppermute(value, 'obs', [(o, o ^ k) for o in range(OBS)])  66.4 us
    pallas_call x1, Pallas kernels, cholesky_parts(): pl.pallas_call(chol_kernel, out_shape=(jax.ShapeDtypeStruct((width, width...  42.1 us
    ppermute x10, waiting for transfers between devices, over_chips(): lax.ppermute(value, 'unk', [(u, u ^ 2 * k) for u in range(UNK)])  27.3 us
    ppermute x10, starting transfers between devices, from_distance(): return lax.ppermute(value, 'obs', [(o, o ^ k) for o in range(OBS)])  23.9 us
    ppermute x10, starting transfers between devices, over_chips(): lax.ppermute(value, 'unk', [(u, u ^ 2 * k) for u in range(UNK)])  20.5 us
    dot_general x4, matrix products, high_dot(): lax.dot_general(left, right, (((0,), (0,)), ((), ())), precision=lax.Prec...  16 us
    ppermute x3, starting transfers between devices, swap_cores(): return lax.ppermute(value, 'unk', [(u, u ^ 1) for u in range(UNK)])  11.6 us
    ppermute x7, starting transfers between devices, local(): lax.ppermute(design[:, j * BLOCK:(j + 1) * BLOCK], BOTH, pairs)  8.77 us
  transfers between devices with their start and end apart: 30, of which 15 were waited for; matrix products, arithmetic and copies ran while one was open for 10% of the time, Pallas kernels for 0%

profile of v1, /device:TPU:7, one launch (start us, length us, event | category | flops | bytes accessed | tf_op | source)
XLA Modules:
  0.0 243.4 jit_solution(6340190456940467892)
XLA Ops:
  0.0 3.1 %fusion.11 = (f32[1024,128]{1,0:T(8,128)S(1)}, f32[1024,128]{1,0:T(8,128)}, f32[1024,128]{1,0:T(8,128)S(1)}, f32[1024,128]{1,0:T(8,128)S(1)}, f32[1024,128]{1,0:...) fusion(f32[1024,1536]{1,0:T(8,128)} %param.2), kind=kLoop, calls=%fused_computation.42 | loop fusion | bytes 7340032 | tf_op jit(solution)/shard_map/slice | solution.py:230
  12.0 5.9 %dynamic-slice_multiply_fusion = (f32[512,1536]{1,0:T(8,128)}, f32[512,1536]{1,0:T(8,128)}) fusion(f32[1024,1536]{1,0:T(8,128)} %param.2, s32[]{:T(128)S(6)} %select_n.117, f32[512]{0:T(512)S(1)} %get-tuple-element.74, f32[512]{0:T(512)S(1)} %get-tuple-element.75, s32[]{:T(128)S(6)} %select_n.116), kind=kLoop, calls=%fused_computation | loop fusion | flops 1572864 | bytes 12587016 | tf_op jit(solution)/shard_map/mul | solution.py:234
  17.9 2.1 add_add_fusion.1
  20.1 8.1 %collective-permute-start.7 = (f32[512,128]{1,0:T(8,128)S(1)}, f32[512,128]{1,0:T(8,128)S(1)}, u32[]{:S(2)}, u32[]{:S(2)}) collective-permute-start(f32[512,128]{1,0:T(8,128)S(1)} %slice.45), channel_id=1, source_target_pairs={{0,1},{1,0},{2,3},{3,2},{4,5},{5,4},{6,7},{7,6},{8,9},{9,8},{10,11... | collective-permute-start | bytes 786440 | tf_op jit(solution)/shard_map/ppermute | solution.py:202
  29.6 5.4 %collective-permute-start.8 = (f32[512,128]{1,0:T(8,128)S(1)}, f32[512,128]{1,0:T(8,128)S(1)}, u32[]{:S(2)}, u32[]{:S(2)}) collective-permute-start(f32[512,128]{1,0:T(8,128)S(1)} %get-tuple-element.50), channel_id=1, source_target_pairs={{0,2},{1,3},{2,0},{3,1},{4,6},{5,7},{6,4},{7,5},{8,10},{9,11},{10,... | collective-permute-start | bytes 786440 | tf_op jit(solution)/shard_map/ppermute | solution.py:207
  35.1 6.3 %collective-permute-start.9 = (f32[512,128]{1,0:T(8,128)S(1)}, f32[512,128]{1,0:T(8,128)S(1)}, u32[]{:S(2)}, u32[]{:S(2)}) collective-permute-start(f32[512,128]{1,0:T(8,128)S(1)} %get-tuple-element.50), channel_id=1, source_target_pairs={{0,4},{1,5},{2,6},{3,7},{4,0},{5,1},{6,2},{7,3},{8,12},{9,13},{10,... | collective-permute-start | bytes 786440 | tf_op jit(solution)/shard_map/ppermute | solution.py:207
  43.4 2.8 %collective-permute-start.13 = (f32[512,128]{1,0:T(8,128)S(1)}, f32[512,128]{1,0:T(8,128)S(1)}, u32[]{:S(2)}, u32[]{:S(2)}) collective-permute-start(f32[512,128]{1,0:T(8,128)S(1)} %get-tuple-element.50), channel_id=1, source_target_pairs={{0,12},{1,13},{2,14},{3,15},{4,8},{5,9},{6,10},{7,11},{8,4},{9,5},... | collective-permute-start | bytes 786440 | tf_op jit(solution)/shard_map/ppermute | solution.py:207
  46.2 7.1 %collective-permute-done.9 = f32[512,128]{1,0:T(8,128)S(1)} collective-permute-done((f32[512,128]{1,0:T(8,128)S(1)}, f32[512,128]{1,0:T(8,128)S(1)}, u32[]{:S(2)}, u32[]{:S(2)}) %collective-permute-start.9) | collective-permute-done | bytes 262176 | tf_op jit(solution)/shard_map/ppermute | solution.py:207
  53.3 2.1 collective-permute-done.10
  55.5 10.3 %collective-permute-done.11 = f32[512,128]{1,0:T(8,128)S(1)} collective-permute-done((f32[512,128]{1,0:T(8,128)S(1)}, f32[512,128]{1,0:T(8,128)S(1)}, u32[]{:S(2)}, u32[]{:S(2)}) %collective-permute-start.11) | collective-permute-done | bytes 262176 | tf_op jit(solution)/shard_map/ppermute | solution.py:207
  69.2 2.8 %collective-permute-done.15 = f32[512,1024]{1,0:T(8,128)} collective-permute-done((f32[512,1024]{1,0:T(8,128)S(1)}, f32[512,1024]{1,0:T(8,128)}, u32[]{:S(2)}, u32[]{:S(2)}) %collective-permute-start.15) | collective-permute-done | bytes 2097184 | tf_op jit(solution)/shard_map/ppermute | solution.py:202
  73.2 2.5 %fusion.4 = f32[128,1024]{1,0:T(8,128)S(1)} fusion(f32[512,1024]{1,0:T(8,128)} %collective-permute-done.15, f32[512,64]{1,0:T(8,128)S(1)} %get-tuple-element.69, f32[512,64]{1,0:T(8,128)S(1)} %get-tuple-element.68, f32[512]{0:T(512)S(1)} %get-tuple-element.74), kind=kOutput, calls=%fused_computation.12 | convolution fusion | flops 402784256 | bytes 2885632 | tf_op jit(solution)/shard_map/dot_general | solution.py:216
  75.9 3.6 %collective-permute-start.16 = (f32[64,1152]{1,0:T(8,128)S(1)}, f32[64,1152]{1,0:T(8,128)S(1)}, u32[]{:S(2)}, u32[]{:S(2)}) collective-permute-start(f32[64,1152]{1,0:T(8,128)S(1)} %fusion), channel_id=1, source_target_pairs={{0,64},{16,80},{32,96},{48,112},{64,0},{80,16},{96,32},{112,48},{1... | collective-permute-start | bytes 884744 | tf_op jit(solution)/shard_map/ppermute | solution.py:212
  79.4 5.5 %fusion.14 = f32[1536,1024]{1,0:T(8,128)S(1)} fusion(f32[512,1536]{1,0:T(8,128)S(1)} %copy-done.1, f32[512,1024]{1,0:T(8,128)S(1)} %constant_dynamic-update-slice_fusion), kind=kOutput, calls=%fused_computation.45 | convolution fusion | flops 4831838208 | bytes 11534336 | tf_op jit(solution)/shard_map/dot_general | solution.py:216
  88.1 7.1 %fusion.15 = f32[1536,1024]{1,0:T(8,128)S(1)} fusion(f32[512,1536]{1,0:T(8,128)S(1)} %copy-done, f32[512,1024]{1,0:T(8,128)} %collective-permute-done.15), kind=kOutput, calls=%fused_computation.46 | convolution fusion | flops 4831838208 | bytes 11534336 | tf_op jit(solution)/shard_map/dot_general | solution.py:216
  95.2 2.2 add.174
  99.0 2.7 %collective-permute-start.25 = (f32[64,1152]{1,0:T(8,128)S(1)}, f32[64,1152]{1,0:T(8,128)S(1)}, u32[]{:S(2)}, u32[]{:S(2)}) collective-permute-start(f32[64,1152]{1,0:T(8,128)S(1)} %add.173), channel_id=1, source_target_pairs={{0,32},{16,48},{32,0},{48,16},{64,96},{80,112},{96,64},{112,80},{1... | collective-permute-start | bytes 884744 | tf_op jit(solution)/shard_map/ppermute | solution.py:212
  101.7 2.3 collective-permute-start.24
  105.7 2.2 collective-permute-done.25
  107.9 2.7 %collective-permute-start.28 = (f32[64,1152]{1,0:T(8,128)S(1)}, f32[64,1152]{1,0:T(8,128)S(1)}, u32[]{:S(2)}, u32[]{:S(2)}) collective-permute-start(f32[64,1152]{1,0:T(8,128)S(1)} %add.190), channel_id=1, source_target_pairs={{0,6},{1,7},{2,4},{3,5},{4,2},{5,3},{6,0},{7,1},{8,14},{9,15},{10,... | collective-permute-start | bytes 884744 | tf_op jit(solution)/shard_map/ppermute | solution.py:207
  110.7 2.3 collective-permute-start.22
  114.2 3.6 %collective-permute-done.28 = f32[64,1152]{1,0:T(8,128)S(1)} collective-permute-done((f32[64,1152]{1,0:T(8,128)S(1)}, f32[64,1152]{1,0:T(8,128)S(1)}, u32[]{:S(2)}, u32[]{:S(2)}) %collective-permute-start.28) | collective-permute-done | bytes 294944 | tf_op jit(solution)/shard_map/ppermute | solution.py:207
  117.7 2.7 %collective-permute-done.27 = f32[64,1152]{1,0:T(8,128)S(1)} collective-permute-done((f32[64,1152]{1,0:T(8,128)S(1)}, f32[64,1152]{1,0:T(8,128)S(1)}, u32[]{:S(2)}, u32[]{:S(2)}) %collective-permute-start.27) | collective-permute-done | bytes 294944 | tf_op jit(solution)/shard_map/ppermute | solution.py:207
  120.4 5.3 %collective-permute-start.21 = (f32[192,1024]{1,0:T(8,128)S(1)}, f32[192,1024]{1,0:T(8,128)S(1)}, u32[]{:S(2)}, u32[]{:S(2)}) collective-permute-start(f32[192,1024]{1,0:T(8,128)S(1)} %get-tuple-element.42), channel_id=1, source_target_pairs={{0,64},{16,80},{32,96},{48,112},{64,0},{80,16},{96,32},{112,48},{1... | collective-permute-start | bytes 2359304 | tf_op jit(solution)/shard_map/ppermute | solution.py:212
  126.2 31.6 %collective-permute-done.24 = f32[192,1024]{1,0:T(8,128)S(1)} collective-permute-done((f32[192,1024]{1,0:T(8,128)S(1)}, f32[192,1024]{1,0:T(8,128)S(1)}, u32[]{:S(2)}, u32[]{:S(2)}) %collective-permute-start.24) | collective-permute-done | bytes 786464 | tf_op jit(solution)/shard_map/ppermute | solution.py:212
  157.8 3.0 %collective-permute-start.19 = (f32[192,1024]{1,0:T(8,128)S(1)}, f32[192,1024]{1,0:T(8,128)S(1)}, u32[]{:S(2)}, u32[]{:S(2)}) collective-permute-start(f32[192,1024]{1,0:T(8,128)S(1)} %get-tuple-element.40), channel_id=1, source_target_pairs={{0,32},{16,48},{32,0},{48,16},{64,96},{80,112},{96,64},{112,80},{1... | collective-permute-start | bytes 2359304 | tf_op jit(solution)/shard_map/ppermute | solution.py:212
  162.1 2.6 %collective-permute-start.29 = (f32[4,64,1152]{2,1,0:T(8,128)S(1)}, f32[4,64,1152]{2,1,0:T(8,128)S(1)}, u32[]{:S(2)}, u32[]{:S(2)}) collective-permute-start(f32[4,64,1152]{2,1,0:T(8,128)S(1)} %pad_maximum_fusion.mine_ref), channel_id=1, source_target_pairs={{0,1},{1,0},{2,3},{3,2},{4,5},{5,4},{6,7},{7,6},{8,9},{9,8},{10,11... | collective-permute-start | bytes 3538952 | tf_op jit(solution)/shard_map/ppermute | solution.py:202
  164.8 14.5 %collective-permute-done.21 = f32[192,1024]{1,0:T(8,128)S(1)} collective-permute-done((f32[192,1024]{1,0:T(8,128)S(1)}, f32[192,1024]{1,0:T(8,128)S(1)}, u32[]{:S(2)}, u32[]{:S(2)}) %collective-permute-start.21) | collective-permute-done | bytes 786464 | tf_op jit(solution)/shard_map/ppermute | solution.py:212
  179.3 8.4 %collective-permute-done.20 = f32[192,1024]{1,0:T(8,128)S(1)} collective-permute-done((f32[192,1024]{1,0:T(8,128)S(1)}, f32[192,1024]{1,0:T(8,128)S(1)}, u32[]{:S(2)}, u32[]{:S(2)}) %collective-permute-start.20) | collective-permute-done | bytes 786464 | tf_op jit(solution)/shard_map/ppermute | solution.py:212
  187.7 8.3 %collective-permute-done.18 = f32[192,1024]{1,0:T(8,128)S(1)} collective-permute-done((f32[192,1024]{1,0:T(8,128)S(1)}, f32[192,1024]{1,0:T(8,128)S(1)}, u32[]{:S(2)}, u32[]{:S(2)}) %collective-permute-start.18) | collective-permute-done | bytes 786464 | tf_op jit(solution)/shard_map/ppermute | solution.py:212
  196.7 42.1 %shard_map.28 = (f32[1024,1024]{1,0:T(8,128)S(1)}, f32[1024,128]{1,0:T(8,128)S(1)}) custom-call(s32[2]{0:T(128)S(1)} %pad_add_fusion.where_ref, f32[4,64,1152]{2,1,0:T(8,128)S(1)} %pad_maximum_fusion.mine_ref, f32[4,64,1152]{2,1,0:T(8,128)S(1)} %collective-permute-done.29.other_ref), custom_call_target="tpu_custom_call" | custom-call | flops 80000000000 | bytes 8388608 | tf_op jit(solution)/shard_map/pallas_call | solution.py:140
  238.8 4.6 %shard_map.29 = f32[192,1024]{1,0:T(8,128)} custom-call(f32[192,1024]{1,0:T(8,128)S(1)} %add_add_fusion.gram_ref, f32[1024,1024]{1,0:T(8,128)S(1)} %get-tuple-element.47.low_ref, f32[1024,128]{1,0:T(8,128)S(1)} %get-tuple-element.48.inv_ref), custom_call_target="tpu_custom_call" | custom-call | tf_op jit(solution)/shard_map/pallas_call | solution.py:177
  (68 shorter events, 27.3 us)
Async XLA Ops:
  0.0 10.5 %copy-start.2 = (f32[1024]{0:T(1024)S(1)}, f32[1024]{0:T(1024)}, u32[]{:S(2)}) copy-start(f32[1024]{0:T(1024)} %param.3) | copy-start | bytes 12292
  3.1 7.5 %collective-permute-start.6 = (f32[1024,128]{1,0:T(8,128)}, f32[1024,128]{1,0:T(8,128)}, u32[]{:S(2)}, u32[]{:S(2)}) collective-permute-start(f32[1024,128]{1,0:T(8,128)} %get-tuple-element.62), channel_id=1, source_target_pairs={{0,14},{16,30},{32,46},{48,62},{64,78},{80,94},{96,110},{112,126}} | collective-permute-start | bytes 1572872 | tf_op jit(solution)/shard_map/ppermute | solution.py:230
  4.6 6.7 %collective-permute-start.5 = (f32[1024,128]{1,0:T(8,128)S(1)}, f32[1024,128]{1,0:T(8,128)}, u32[]{:S(2)}, u32[]{:S(2)}) collective-permute-start(f32[1024,128]{1,0:T(8,128)S(1)} %get-tuple-element.63), channel_id=1, source_target_pairs={{0,12},{16,28},{32,44},{48,60},{64,76},{80,92},{96,108},{112,124}} | collective-permute-start | bytes 1572872 | tf_op jit(solution)/shard_map/ppermute | solution.py:230
  6.0 11.9 %collective-permute-start.4 = (f32[1024,128]{1,0:T(8,128)S(1)}, f32[1024,128]{1,0:T(8,128)}, u32[]{:S(2)}, u32[]{:S(2)}) collective-permute-start(f32[1024,128]{1,0:T(8,128)S(1)} %get-tuple-element.64), channel_id=1, source_target_pairs={{0,10},{16,26},{32,42},{48,58},{64,74},{80,90},{96,106},{112,122}} | collective-permute-start | bytes 1572872 | tf_op jit(solution)/shard_map/ppermute | solution.py:230
  7.5 10.4 %collective-permute-start.3 = (f32[1024,128]{1,0:T(8,128)S(1)}, f32[1024,128]{1,0:T(8,128)}, u32[]{:S(2)}, u32[]{:S(2)}) collective-permute-start(f32[1024,128]{1,0:T(8,128)S(1)} %get-tuple-element.65), channel_id=1, source_target_pairs={{0,8},{16,24},{32,40},{48,56},{64,72},{80,88},{96,104},{112,120}} | collective-permute-start | bytes 1572872 | tf_op jit(solution)/shard_map/ppermute | solution.py:230
  9.0 8.9 %collective-permute-start.2 = (f32[1024,128]{1,0:T(8,128)S(1)}, f32[1024,128]{1,0:T(8,128)}, u32[]{:S(2)}, u32[]{:S(2)}) collective-permute-start(f32[1024,128]{1,0:T(8,128)S(1)} %get-tuple-element.66), channel_id=1, source_target_pairs={{0,6},{16,22},{32,38},{48,54},{64,70},{80,86},{96,102},{112,118}} | collective-permute-start | bytes 1572872 | tf_op jit(solution)/shard_map/ppermute | solution.py:230
  10.6 7.3 %collective-permute-start.1 = (f32[1024,128]{1,0:T(8,128)S(1)}, f32[1024,128]{1,0:T(8,128)S(1)}, u32[]{:S(2)}, u32[]{:S(2)}) collective-permute-start(f32[1024,128]{1,0:T(8,128)S(1)} %get-tuple-element.67), channel_id=1, source_target_pairs={{0,4},{16,20},{32,36},{48,52},{64,68},{80,84},{96,100},{112,116}} | collective-permute-start | bytes 1572872 | tf_op jit(solution)/shard_map/ppermute | solution.py:230
  11.3 6.6 %collective-permute-start = (f32[1024,128]{1,0:T(8,128)S(1)}, f32[1024,128]{1,0:T(8,128)S(1)}, u32[]{:S(2)}, u32[]{:S(2)}) collective-permute-start(f32[1024,128]{1,0:T(8,128)S(1)} %get-tuple-element.61), channel_id=1, source_target_pairs={{0,2},{16,18},{32,34},{48,50},{64,66},{80,82},{96,98},{112,114}} | collective-permute-start | bytes 1572872 | tf_op jit(solution)/shard_map/ppermute | solution.py:230
  20.1 9.3 %collective-permute-start.7 = (f32[512,128]{1,0:T(8,128)S(1)}, f32[512,128]{1,0:T(8,128)S(1)}, u32[]{:S(2)}, u32[]{:S(2)}) collective-permute-start(f32[512,128]{1,0:T(8,128)S(1)} %slice.45), channel_id=1, source_target_pairs={{0,1},{1,0},{2,3},{3,2},{4,5},{5,4},{6,7},{7,6},{8,9},{9,8},{10,11... | collective-permute-start | bytes 786440 | tf_op jit(solution)/shard_map/ppermute | solution.py:202
  29.6 13.7 %collective-permute-start.8 = (f32[512,128]{1,0:T(8,128)S(1)}, f32[512,128]{1,0:T(8,128)S(1)}, u32[]{:S(2)}, u32[]{:S(2)}) collective-permute-start(f32[512,128]{1,0:T(8,128)S(1)} %get-tuple-element.50), channel_id=1, source_target_pairs={{0,2},{1,3},{2,0},{3,1},{4,6},{5,7},{6,4},{7,5},{8,10},{9,11},{10,... | collective-permute-start | bytes 786440 | tf_op jit(solution)/shard_map/ppermute | solution.py:207
  35.1 18.2 %collective-permute-start.9 = (f32[512,128]{1,0:T(8,128)S(1)}, f32[512,128]{1,0:T(8,128)S(1)}, u32[]{:S(2)}, u32[]{:S(2)}) collective-permute-start(f32[512,128]{1,0:T(8,128)S(1)} %get-tuple-element.50), channel_id=1, source_target_pairs={{0,4},{1,5},{2,6},{3,7},{4,0},{5,1},{6,2},{7,3},{8,12},{9,13},{10,... | collective-permute-start | bytes 786440 | tf_op jit(solution)/shard_map/ppermute | solution.py:207
  41.4 14.0 %collective-permute-start.10 = (f32[512,128]{1,0:T(8,128)S(1)}, f32[512,128]{1,0:T(8,128)S(1)}, u32[]{:S(2)}, u32[]{:S(2)}) collective-permute-start(f32[512,128]{1,0:T(8,128)S(1)} %get-tuple-element.50), channel_id=1, source_target_pairs={{0,6},{1,7},{2,4},{3,5},{4,2},{5,3},{6,0},{7,1},{8,14},{9,15},{10,... | collective-permute-start | bytes 786440 | tf_op jit(solution)/shard_map/ppermute | solution.py:207
  41.6 24.2 %collective-permute-start.11 = (f32[512,128]{1,0:T(8,128)S(1)}, f32[512,128]{1,0:T(8,128)S(1)}, u32[]{:S(2)}, u32[]{:S(2)}) collective-permute-start(f32[512,128]{1,0:T(8,128)S(1)} %get-tuple-element.50), channel_id=1, source_target_pairs={{0,8},{1,9},{2,10},{3,11},{4,12},{5,13},{6,14},{7,15},{8,0},{9,1},... | collective-permute-start | bytes 786440 | tf_op jit(solution)/shard_map/ppermute | solution.py:207
  41.6 24.2 %collective-permute-start.12 = (f32[512,128]{1,0:T(8,128)S(1)}, f32[512,128]{1,0:T(8,128)S(1)}, u32[]{:S(2)}, u32[]{:S(2)}) collective-permute-start(f32[512,128]{1,0:T(8,128)S(1)} %get-tuple-element.50), channel_id=1, source_target_pairs={{0,10},{1,11},{2,8},{3,9},{4,14},{5,15},{6,12},{7,13},{8,2},{9,3},... | collective-permute-start | bytes 786440 | tf_op jit(solution)/shard_map/ppermute | solution.py:207
  43.4 22.5 %collective-permute-start.13 = (f32[512,128]{1,0:T(8,128)S(1)}, f32[512,128]{1,0:T(8,128)S(1)}, u32[]{:S(2)}, u32[]{:S(2)}) collective-permute-start(f32[512,128]{1,0:T(8,128)S(1)} %get-tuple-element.50), channel_id=1, source_target_pairs={{0,12},{1,13},{2,14},{3,15},{4,8},{5,9},{6,10},{7,11},{8,4},{9,5},... | collective-permute-start | bytes 786440 | tf_op jit(solution)/shard_map/ppermute | solution.py:207
  53.3 13.8 %collective-permute-start.14 = (f32[512,128]{1,0:T(8,128)S(1)}, f32[512,128]{1,0:T(8,128)S(1)}, u32[]{:S(2)}, u32[]{:S(2)}) collective-permute-start(f32[512,128]{1,0:T(8,128)S(1)} %get-tuple-element.50), channel_id=1, source_target_pairs={{0,14},{1,15},{2,12},{3,13},{4,10},{5,11},{6,8},{7,9},{8,6},{9,7},... | collective-permute-start | bytes 786440 | tf_op jit(solution)/shard_map/ppermute | solution.py:207
  67.1 4.8 %collective-permute-start.15 = (f32[512,1024]{1,0:T(8,128)S(1)}, f32[512,1024]{1,0:T(8,128)}, u32[]{:S(2)}, u32[]{:S(2)}) collective-permute-start(f32[512,1024]{1,0:T(8,128)S(1)} %constant_dynamic-update-slice_fusion), channel_id=1, source_target_pairs={{0,1},{1,0},{2,3},{3,2},{4,5},{5,4},{6,7},{7,6},{8,9},{9,8},{10,11... | collective-permute-start | bytes 6291464 | tf_op jit(solution)/shard_map/ppermute | solution.py:202
  75.9 10.6 %collective-permute-start.16 = (f32[64,1152]{1,0:T(8,128)S(1)}, f32[64,1152]{1,0:T(8,128)S(1)}, u32[]{:S(2)}, u32[]{:S(2)}) collective-permute-start(f32[64,1152]{1,0:T(8,128)S(1)} %fusion), channel_id=1, source_target_pairs={{0,64},{16,80},{32,96},{48,112},{64,0},{80,16},{96,32},{112,48},{1... | collective-permute-start | bytes 884744 | tf_op jit(solution)/shard_map/ppermute | solution.py:212
  79.4 8.6 %copy-start = (f32[512,1536]{1,0:T(8,128)S(1)}, f32[512,1536]{1,0:T(8,128)}, u32[]{:S(2)}) copy-start(f32[512,1536]{1,0:T(8,128)} %get-tuple-element.36) | copy-start | bytes 9437188
  86.5 11.5 %collective-permute-start.17 = (f32[64,1152]{1,0:T(8,128)S(1)}, f32[64,1152]{1,0:T(8,128)}, u32[]{:S(2)}, u32[]{:S(2)}) collective-permute-start(f32[64,1152]{1,0:T(8,128)S(1)} %add.172), channel_id=1, source_target_pairs={{0,16},{16,0},{32,48},{48,32},{64,80},{80,64},{96,112},{112,96},{1... | collective-permute-start | bytes 884744 | tf_op jit(solution)/shard_map/ppermute | solution.py:212
  99.0 8.9 %collective-permute-start.25 = (f32[64,1152]{1,0:T(8,128)S(1)}, f32[64,1152]{1,0:T(8,128)S(1)}, u32[]{:S(2)}, u32[]{:S(2)}) collective-permute-start(f32[64,1152]{1,0:T(8,128)S(1)} %add.173), channel_id=1, source_target_pairs={{0,32},{16,48},{32,0},{48,16},{64,96},{80,112},{96,64},{112,80},{1... | collective-permute-start | bytes 884744 | tf_op jit(solution)/shard_map/ppermute | solution.py:212
  101.7 56.1 %collective-permute-start.24 = (f32[192,1024]{1,0:T(8,128)S(1)}, f32[192,1024]{1,0:T(8,128)S(1)}, u32[]{:S(2)}, u32[]{:S(2)}) collective-permute-start(f32[192,1024]{1,0:T(8,128)S(1)} %get-tuple-element.45), channel_id=1, source_target_pairs={{0,112},{16,96},{32,80},{48,64},{64,48},{80,32},{96,16},{112,0},{1... | collective-permute-start | bytes 2359304 | tf_op jit(solution)/shard_map/ppermute | solution.py:212
  104.0 56.8 %collective-permute-start.23 = (f32[192,1024]{1,0:T(8,128)S(1)}, f32[192,1024]{1,0:T(8,128)S(1)}, u32[]{:S(2)}, u32[]{:S(2)}) collective-permute-start(f32[192,1024]{1,0:T(8,128)S(1)} %get-tuple-element.44), channel_id=1, source_target_pairs={{0,96},{16,112},{32,64},{48,80},{64,32},{80,48},{96,0},{112,16},{1... | collective-permute-start | bytes 2359304 | tf_op jit(solution)/shard_map/ppermute | solution.py:212
  107.9 9.8 %collective-permute-start.28 = (f32[64,1152]{1,0:T(8,128)S(1)}, f32[64,1152]{1,0:T(8,128)S(1)}, u32[]{:S(2)}, u32[]{:S(2)}) collective-permute-start(f32[64,1152]{1,0:T(8,128)S(1)} %add.190), channel_id=1, source_target_pairs={{0,6},{1,7},{2,4},{3,5},{4,2},{5,3},{6,0},{7,1},{8,14},{9,15},{10,... | collective-permute-start | bytes 884744 | tf_op jit(solution)/shard_map/ppermute | solution.py:207
  110.7 51.4 %collective-permute-start.22 = (f32[192,1024]{1,0:T(8,128)S(1)}, f32[192,1024]{1,0:T(8,128)S(1)}, u32[]{:S(2)}, u32[]{:S(2)}) collective-permute-start(f32[192,1024]{1,0:T(8,128)S(1)} %get-tuple-element.43), channel_id=1, source_target_pairs={{0,80},{16,64},{32,112},{48,96},{64,16},{80,0},{96,48},{112,32},{1... | collective-permute-start | bytes 2359304 | tf_op jit(solution)/shard_map/ppermute | solution.py:212
  113.0 7.4 %collective-permute-start.27 = (f32[64,1152]{1,0:T(8,128)S(1)}, f32[64,1152]{1,0:T(8,128)S(1)}, u32[]{:S(2)}, u32[]{:S(2)}) collective-permute-start(f32[64,1152]{1,0:T(8,128)S(1)} %add.190), channel_id=1, source_target_pairs={{0,4},{1,5},{2,6},{3,7},{4,0},{5,1},{6,2},{7,3},{8,12},{9,13},{10,... | collective-permute-start | bytes 884744 | tf_op jit(solution)/shard_map/ppermute | solution.py:207
  117.7 8.3 %collective-permute-start.26 = (f32[64,1152]{1,0:T(8,128)S(1)}, f32[64,1152]{1,0:T(8,128)S(1)}, u32[]{:S(2)}, u32[]{:S(2)}) collective-permute-start(f32[64,1152]{1,0:T(8,128)S(1)} %add.190), channel_id=1, source_target_pairs={{0,2},{1,3},{2,0},{3,1},{4,6},{5,7},{6,4},{7,5},{8,10},{9,11},{10,... | collective-permute-start | bytes 884744 | tf_op jit(solution)/shard_map/ppermute | solution.py:207
  120.4 58.9 %collective-permute-start.21 = (f32[192,1024]{1,0:T(8,128)S(1)}, f32[192,1024]{1,0:T(8,128)S(1)}, u32[]{:S(2)}, u32[]{:S(2)}) collective-permute-start(f32[192,1024]{1,0:T(8,128)S(1)} %get-tuple-element.42), channel_id=1, source_target_pairs={{0,64},{16,80},{32,96},{48,112},{64,0},{80,16},{96,32},{112,48},{1... | collective-permute-start | bytes 2359304 | tf_op jit(solution)/shard_map/ppermute | solution.py:212
  126.1 61.6 %collective-permute-start.20 = (f32[192,1024]{1,0:T(8,128)S(1)}, f32[192,1024]{1,0:T(8,128)S(1)}, u32[]{:S(2)}, u32[]{:S(2)}) collective-permute-start(f32[192,1024]{1,0:T(8,128)S(1)} %get-tuple-element.41), channel_id=1, source_target_pairs={{0,48},{16,32},{32,16},{48,0},{64,112},{80,96},{96,80},{112,64},{1... | collective-permute-start | bytes 2359304 | tf_op jit(solution)/shard_map/ppermute | solution.py:212
  157.8 29.9 %collective-permute-start.19 = (f32[192,1024]{1,0:T(8,128)S(1)}, f32[192,1024]{1,0:T(8,128)S(1)}, u32[]{:S(2)}, u32[]{:S(2)}) collective-permute-start(f32[192,1024]{1,0:T(8,128)S(1)} %get-tuple-element.40), channel_id=1, source_target_pairs={{0,32},{16,48},{32,0},{48,16},{64,96},{80,112},{96,64},{112,80},{1... | collective-permute-start | bytes 2359304 | tf_op jit(solution)/shard_map/ppermute | solution.py:212
  160.8 35.2 %collective-permute-start.18 = (f32[192,1024]{1,0:T(8,128)S(1)}, f32[192,1024]{1,0:T(8,128)S(1)}, u32[]{:S(2)}, u32[]{:S(2)}) collective-permute-start(f32[192,1024]{1,0:T(8,128)S(1)} %get-tuple-element.39), channel_id=1, source_target_pairs={{0,16},{16,0},{32,48},{48,32},{64,80},{80,64},{96,112},{112,96},{1... | collective-permute-start | bytes 2359304 | tf_op jit(solution)/shard_map/ppermute | solution.py:212
  162.1 34.6 %collective-permute-start.29 = (f32[4,64,1152]{2,1,0:T(8,128)S(1)}, f32[4,64,1152]{2,1,0:T(8,128)S(1)}, u32[]{:S(2)}, u32[]{:S(2)}) collective-permute-start(f32[4,64,1152]{2,1,0:T(8,128)S(1)} %pad_maximum_fusion.mine_ref), channel_id=1, source_target_pairs={{0,1},{1,0},{2,3},{3,2},{4,5},{5,4},{6,7},{7,6},{8,9},{9,8},{10,11... | collective-permute-start | bytes 3538952 | tf_op jit(solution)/shard_map/ppermute | solution.py:202
  (1 other events, 3.8 us)
